TPU v7x, 1024 devices: a whole 4x4x32 slice. The times are simulated.
1024 devices in a mesh: dp: 4 (over y), expert: 32 (over x, z_hi, core), tensor: 8 (over z_lo).
Axes of the slice: x: 4, y: 4, z: 32 (z_hi: 4, z_lo: 8; z = z_hi * 8 + z_lo), core: 2. Of those that a mesh axis runs over, the one named last changes fastest.
Arguments:
- hidden: bfloat16 [16384, 2048], P(('dp', 'expert')), may hold values from -6 to 6
- out_grad: bfloat16 [16384, 7168], P(('dp', 'expert'), 'tensor'), may hold values from -6 to 6
- w_down: bfloat16 [32, 2048, 7168], P('expert', None, 'tensor'), may hold values from -0.125 to 0.125
- routes: int32 [16384, 1], P(('dp', 'expert')), may hold values from 0 to 31; in each aligned block of 128 rows (0 to 127, 128 to 255, ...) at most 8 rows name the same one
- placement: int32 [32], replicated, may hold values from 0 to 31, as said below
Outputs:
- output: bfloat16 [16384, 7168], P(('dp', 'expert'), 'tensor')
- d_hidden: bfloat16 [16384, 2048], P(('dp', 'expert'), 'tensor')
- d_weight: bfloat16 [32, 2048, 7168], P('expert', 'dp', 'tensor')
Inputs may be any that keep to these rules, and one draw needn't show every extreme that they name: `routes`: among the 128 tokens of one index pair of dp and expert, no expert is named more than 8 times, a bound that some block reaches. `placement`: each expert is held at exactly one index.
All inputs are finite; a program needn't handle non-finite values.
Results may differ from a plain program's by a relative error of at most 0.009.
Values may be sent and summed in bfloat16 or wider, within the bound.
A program may use at most 32 MiB of HBM per device.

v0:
```python
import jax
import jax.numpy as jnp
from jax import lax
from jax.sharding import PartitionSpec as P


def shards(hidden, out_grad, w_down, routes, placement):
    experts = lax.axis_size("expert")
    tok = hidden.shape[0]
    cols = out_grad.shape[1]
    cap = 2 * tok // experts
    slots = experts * cap
    chosen = routes == jnp.arange(placement.shape[0], dtype=jnp.int32)[None, :]
    target = jnp.sum(jnp.where(chosen, placement[None, :], 0), axis=1)
    landing = target[:, None] == jnp.arange(experts, dtype=jnp.int32)[None, :]
    counted = jnp.cumsum(landing.astype(jnp.int32), axis=0) - 1
    within = jnp.sum(jnp.where(landing, counted, 0), axis=1)
    position = target * cap + within
    picker = (jnp.arange(slots, dtype=jnp.int32)[:, None] == position[None, :]).astype(jnp.bfloat16)
    send_hidden = jnp.dot(picker, hidden, preferred_element_type=jnp.float32).astype(jnp.bfloat16)
    send_grad = jnp.dot(picker, out_grad, preferred_element_type=jnp.float32).astype(jnp.bfloat16)
    recv_hidden, recv_grad = (
        lax.all_to_all(
            send_hidden.reshape(experts, cap, -1), "expert", split_axis=0, concat_axis=0, tiled=True
        ),
        lax.all_to_all(
            send_grad.reshape(experts, cap, cols), "expert", split_axis=0, concat_axis=0, tiled=True
        ),
    )
    slot_hidden = recv_hidden.reshape(slots, -1)
    slot_grad = recv_grad.reshape(slots, cols)
    weight = w_down[0]
    out_rows = jnp.dot(slot_hidden, weight, preferred_element_type=jnp.float32).astype(jnp.bfloat16)
    partial_value = lax.dot_general(
        slot_grad, weight, (((1,), (1,)), ((), ())), preferred_element_type=jnp.float32
    )
    hidden_grad = lax.psum_scatter(partial_value, "tensor", scatter_dimension=1, tiled=True).astype(
        jnp.bfloat16
    )
    back_out, back_grad = (
        lax.all_to_all(
            out_rows.reshape(experts, cap, cols), "expert", split_axis=0, concat_axis=0, tiled=True
        ),
        lax.all_to_all(
            hidden_grad.reshape(experts, cap, -1), "expert", split_axis=0, concat_axis=0, tiled=True
        ),
    )
    output = jnp.einsum(
        "rt,rd->td", picker, back_out.reshape(slots, cols), preferred_element_type=jnp.float32
    ).astype(jnp.bfloat16)
    d_hidden = jnp.einsum(
        "rt,rd->td", picker, back_grad.reshape(slots, -1), preferred_element_type=jnp.float32
    ).astype(jnp.bfloat16)
    summed = lax.psum_scatter(
        lax.dot_general(
            slot_hidden, slot_grad, (((0,), (0,)), ((), ())), preferred_element_type=jnp.float32
        ).astype(jnp.bfloat16),
        "dp",
        scatter_dimension=0,
        tiled=True,
    )
    d_weight = summed[None]
    return (output, d_hidden, d_weight)


def solution(mesh):
    in_specs = (
        P(("dp", "expert"), None),
        P(("dp", "expert"), "tensor"),
        P("expert", None, "tensor"),
        P(("dp", "expert"), None),
        P(),
    )
    out_specs = (
        P(("dp", "expert"), "tensor"),
        P(("dp", "expert"), "tensor"),
        P("expert", "dp", "tensor"),
    )
    return jax.shard_map(shards, mesh=mesh, in_specs=in_specs, out_specs=out_specs, check_vma=False)
```

profile of v0, /device:TPU:40, one launch (start us, length us, event | category | flops | bytes accessed | tf_op | source)
XLA Modules:
  0.0 365.8 jit_solution(16977635747540612697)
XLA Ops:
  7.2 0.0 copy-start
  7.2 0.9 select_reduce_fusion.1
  8.1 0.1 fusion.20
  8.2 0.2 reduce_window_sum.11
  8.4 0.2 select_reduce_fusion
  8.5 2.0 fusion.8
  10.5 30.3 %all-to-all-start.2 = ((bf16[32,8,896]{2,1,0:T(8,128)(2,1)}), bf16[32,8,896]{2,1,0:T(8,128)(2,1)S(1)}, u32[]{:S(2)}, u32[]{:S(2)}) async-start(bf16[32,8,896]{2,1,0:T(8,128)(2,1)} %fusion.8), calls=%async_computation.2 | async-start | bytes 917504 | tf_op jit(solution)/shard_map/all_to_all | solution.py:26
  40.8 0.0 copy-done
  40.8 1.4 fusion.4
  42.2 59.9 %all-to-all-done.2 = bf16[32,8,896]{2,1,0:T(8,128)(2,1)S(1)} async-done(((bf16[32,8,896]{2,1,0:T(8,128)(2,1)}), bf16[32,8,896]{2,1,0:T(8,128)(2,1)S(1)}, u32[]{:S(2)}, u32[]{:S(2)}) %all-to-all-start.2) | async-done | bytes 458784 | tf_op jit(solution)/shard_map/all_to_all | solution.py:26
  102.1 3.9 %all-to-all-start = ((bf16[32,8,2048]{2,1,0:T(8,128)(2,1)}), bf16[32,8,2048]{2,1,0:T(8,128)(2,1)S(1)}, u32[]{:S(2)}, u32[]{:S(2)}) async-start(bf16[32,8,2048]{2,1,0:T(8,128)(2,1)} %fusion.4), calls=%async_computation | async-start | bytes 2097152 | tf_op jit(solution)/shard_map/all_to_all | solution.py:23
  106.1 0.0 reduce-scatter.3.cloned.1.call-start
  106.1 4.7 %fusion = f32[256,2048]{1,0:T(8,128)} fusion(bf16[1,2048,896]{2,1,0:T(8,128)(2,1)} %param.7, bf16[32,8,896]{2,1,0:T(8,128)(2,1)S(1)} %all-to-all-done.2), kind=kOutput, calls=%fused_computation.1 | convolution fusion | flops 939524096 | bytes 6225920 | tf_op jit(solution)/shard_map/dot_general | solution.py:34
  110.8 0.0 reduce-scatter.3.cloned.1.call-update
  110.8 0.0 reduce-scatter.5.cloned.1.call-start
  110.8 88.1 %all-to-all-done = bf16[32,8,2048]{2,1,0:T(8,128)(2,1)S(1)} async-done(((bf16[32,8,2048]{2,1,0:T(8,128)(2,1)}), bf16[32,8,2048]{2,1,0:T(8,128)(2,1)S(1)}, u32[]{:S(2)}, u32[]{:S(2)}) %all-to-all-start) | async-done | bytes 1048608 | tf_op jit(solution)/shard_map/all_to_all | solution.py:23
  198.9 3.1 bitcast_convert_fusion
  202.0 0.0 reduce-scatter.5.cloned.1.call-update
  202.1 36.2 %reduce-scatter.3.cloned.1.call-done = f32[256,256]{1,0:T(8,128)} async-done(((f32[256,2048]{1,0:T(8,128)}), f32[256,256]{1,0:T(8,128)}) %reduce-scatter.3.cloned.1.call-update) | async-done | bytes 262160 | tf_op jit(solution)/shard_map/reduce_scatter | solution.py:37
  238.3 1.6 convert_bitcast_fusion
  239.9 23.8 %all-to-all-start.3 = ((bf16[32,8,256]{2,1,0:T(8,128)(2,1)}), bf16[32,8,256]{2,1,0:T(8,128)(2,1)S(1)}, u32[]{:S(2)}, u32[]{:S(2)}) async-start(bf16[32,8,256]{2,1,0:T(8,128)(2,1)} %convert_bitcast_fusion), calls=%async_computation.4 | async-start | bytes 262144 | tf_op jit(solution)/shard_map/all_to_all | solution.py:44
  263.7 4.1 %fusion.9 = bf16[32,8,896]{2,1,0:T(8,128)(2,1)} fusion(bf16[1,2048,896]{2,1,0:T(8,128)(2,1)} %param.7, bf16[32,8,2048]{2,1,0:T(8,128)(2,1)S(1)} %all-to-all-done), kind=kOutput, calls=%fused_computation.10 | convolution fusion | flops 939753472 | bytes 5177344 | tf_op jit(solution)/shard_map/dot_general | solution.py:33
  267.8 29.5 %all-to-all-done.3 = bf16[32,8,256]{2,1,0:T(8,128)(2,1)S(1)} async-done(((bf16[32,8,256]{2,1,0:T(8,128)(2,1)}), bf16[32,8,256]{2,1,0:T(8,128)(2,1)S(1)}, u32[]{:S(2)}, u32[]{:S(2)}) %all-to-all-start.3) | async-done | bytes 131104 | tf_op jit(solution)/shard_map/all_to_all | solution.py:44
  297.3 3.9 %all-to-all-start.1 = ((bf16[32,8,896]{2,1,0:T(8,128)(2,1)}), bf16[32,8,896]{2,1,0:T(8,128)(2,1)S(1)}, u32[]{:S(2)}, u32[]{:S(2)}) async-start(bf16[32,8,896]{2,1,0:T(8,128)(2,1)} %fusion.9), calls=%async_computation.1 | async-start | bytes 917504 | tf_op jit(solution)/shard_map/all_to_all | solution.py:41
  301.2 0.9 convolution_convert_fusion.3
  302.0 55.9 %all-to-all-done.1 = bf16[32,8,896]{2,1,0:T(8,128)(2,1)S(1)} async-done(((bf16[32,8,896]{2,1,0:T(8,128)(2,1)}), bf16[32,8,896]{2,1,0:T(8,128)(2,1)S(1)}, u32[]{:S(2)}, u32[]{:S(2)}) %all-to-all-start.1) | async-done | bytes 458784 | tf_op jit(solution)/shard_map/all_to_all | solution.py:41
  358.0 1.0 convolution_convert_fusion.2
  358.9 0.0 reduce-scatter.5.cloned.1.call-done
  (1 shorter events, 0.0 us)
Async XLA Ops:
  7.2 33.7 %copy-start = (bf16[128,2048]{1,0:T(8,128)(2,1)S(1)}, bf16[128,2048]{1,0:T(8,128)(2,1)}, u32[]{:S(2)}) copy-start(bf16[128,2048]{1,0:T(8,128)(2,1)} %param.5) | copy-start | bytes 1572868
  10.5 91.6 %all-to-all-start.2 = ((bf16[32,8,896]{2,1,0:T(8,128)(2,1)}), bf16[32,8,896]{2,1,0:T(8,128)(2,1)S(1)}, u32[]{:S(2)}, u32[]{:S(2)}) async-start(bf16[32,8,896]{2,1,0:T(8,128)(2,1)} %fusion.8), calls=%async_computation.2 | async-start | bytes 917504 | tf_op jit(solution)/shard_map/all_to_all | solution.py:26
  102.1 96.8 %all-to-all-start = ((bf16[32,8,2048]{2,1,0:T(8,128)(2,1)}), bf16[32,8,2048]{2,1,0:T(8,128)(2,1)S(1)}, u32[]{:S(2)}, u32[]{:S(2)}) async-start(bf16[32,8,2048]{2,1,0:T(8,128)(2,1)} %fusion.4), calls=%async_computation | async-start | bytes 2097152 | tf_op jit(solution)/shard_map/all_to_all | solution.py:23
  106.1 132.2 %reduce-scatter.3.cloned.1.call-start = ((), (), s32[]{:S(2)}) async-start(), calls=%async_computation.6 | async-start | bytes 2359296 | tf_op jit(solution)/shard_map/reduce_scatter | solution.py:37
  110.8 248.1 %reduce-scatter.5.cloned.1.call-start = ((), (), s32[]{:S(2)}) async-start(), calls=%async_computation.7 | async-start | bytes 4587520 | tf_op jit(solution)/shard_map/reduce_scatter | solution.py:54
  239.9 57.4 %all-to-all-start.3 = ((bf16[32,8,256]{2,1,0:T(8,128)(2,1)}), bf16[32,8,256]{2,1,0:T(8,128)(2,1)S(1)}, u32[]{:S(2)}, u32[]{:S(2)}) async-start(bf16[32,8,256]{2,1,0:T(8,128)(2,1)} %convert_bitcast_fusion), calls=%async_computation.4 | async-start | bytes 262144 | tf_op jit(solution)/shard_map/all_to_all | solution.py:44
  297.3 60.7 %all-to-all-start.1 = ((bf16[32,8,896]{2,1,0:T(8,128)(2,1)}), bf16[32,8,896]{2,1,0:T(8,128)(2,1)S(1)}, u32[]{:S(2)}, u32[]{:S(2)}) async-start(bf16[32,8,896]{2,1,0:T(8,128)(2,1)} %fusion.9), calls=%async_computation.1 | async-start | bytes 917504 | tf_op jit(solution)/shard_map/all_to_all | solution.py:41
Sparse Core Ops, SparseCore 0:
  110.9 127.2 reduce-scatter.2
  242.3 62.7 reduce-scatter.4
where the time goes:
time: 366 us
  waiting for transfers between devices  270 us (74%)
  starting transfers between devices  62 us (17%)
  matrix products  17.1 us (5%)
  between operations  14.1 us (4%)
    all_to_all x1, waiting for transfers between devices, shards(): lax.all_to_all(send_hidden.reshape(experts, cap, -1), 'expert', split_axi...  88.1 us
    all_to_all x1, waiting for transfers between devices, shards(): lax.all_to_all(send_grad.reshape(experts, cap, cols), 'expert', split_axi...  59.9 us
    all_to_all x1, waiting for transfers between devices, shards(): lax.all_to_all(out_rows.reshape(experts, cap, cols), 'expert', split_axis...  55.9 us
    reduce_scatter x1, waiting for transfers between devices, shards(): lax.psum_scatter(partial_value, 'tensor', scatter_dimension=1, tiled=True)  36.2 us
    all_to_all x1, starting transfers between devices, shards(): lax.all_to_all(send_grad.reshape(experts, cap, cols), 'expert', split_axi...  30.3 us
    all_to_all x1, waiting for transfers between devices, shards(): lax.all_to_all(hidden_grad.reshape(experts, cap, -1), 'expert', split_axi...  29.5 us
    all_to_all x1, starting transfers between devices, shards(): lax.all_to_all(hidden_grad.reshape(experts, cap, -1), 'expert', split_axi...  23.8 us
  transfers between devices with their start and end apart: 6, of which 5 were waited for; matrix products, arithmetic and copies ran while one was open for 5% of the time, Pallas kernels for 0%

commit v1 on v0

v1 whole, which is shorter than its diff:
```python
import jax
import jax.numpy as jnp
from jax import lax
from jax.sharding import PartitionSpec as P


def shards(hidden, out_grad, w_down, routes, placement):
    experts = lax.axis_size("expert")
    parts = lax.axis_size("tensor")
    tok = hidden.shape[0]
    width = hidden.shape[1]
    part = width // parts
    cols = out_grad.shape[1]
    cap = 2 * tok // experts
    slots = experts * cap
    chosen = routes == jnp.arange(placement.shape[0], dtype=jnp.int32)[None, :]
    target = jnp.sum(jnp.where(chosen, placement[None, :], 0), axis=1)
    landing = target[:, None] == jnp.arange(experts, dtype=jnp.int32)[None, :]
    counted = jnp.cumsum(landing.astype(jnp.int32), axis=0) - 1
    within = jnp.sum(jnp.where(landing, counted, 0), axis=1)
    position = target * cap + within
    picker = (jnp.arange(slots, dtype=jnp.int32)[:, None] == position[None, :]).astype(jnp.bfloat16)
    mine = lax.dynamic_slice_in_dim(hidden, lax.axis_index("tensor") * part, part, axis=1)
    rows = jnp.concatenate([out_grad, mine], axis=1)
    send = jnp.dot(picker, rows, preferred_element_type=jnp.float32).astype(jnp.bfloat16)
    recv = lax.all_to_all(
        send.reshape(experts, cap, -1), "expert", split_axis=0, concat_axis=0, tiled=True
    ).reshape(slots, -1)
    slot_grad = recv[:, :cols]
    pieces = lax.all_gather(recv[:, cols:], "tensor", axis=0, tiled=False)
    slot_hidden = pieces.transpose(1, 0, 2).reshape(slots, width)
    weight = w_down[0]
    partial_value = lax.dot_general(
        slot_grad, weight, (((1,), (1,)), ((), ())), preferred_element_type=jnp.float32
    ).astype(jnp.bfloat16)
    hidden_grad = lax.psum_scatter(partial_value, "tensor", scatter_dimension=1, tiled=True)
    out_rows = jnp.dot(slot_hidden, weight, preferred_element_type=jnp.float32).astype(jnp.bfloat16)
    back = lax.all_to_all(
        jnp.concatenate([out_rows, hidden_grad], axis=1).reshape(experts, cap, -1),
        "expert",
        split_axis=0,
        concat_axis=0,
        tiled=True,
    ).reshape(slots, -1)
    final = jnp.einsum("rt,rd->td", picker, back, preferred_element_type=jnp.float32).astype(jnp.bfloat16)
    output = final[:, :cols]
    d_hidden = final[:, cols:]
    summed = lax.psum_scatter(
        lax.dot_general(
            slot_hidden, slot_grad, (((0,), (0,)), ((), ())), preferred_element_type=jnp.float32
        ).astype(jnp.bfloat16),
        "dp",
        scatter_dimension=0,
        tiled=True,
    )
    d_weight = summed[None]
    return (output, d_hidden, d_weight)


def solution(mesh):
    in_specs = (
        P(("dp", "expert"), None),
        P(("dp", "expert"), "tensor"),
        P("expert", None, "tensor"),
        P(("dp", "expert"), None),
        P(),
    )
    out_specs = (
        P(("dp", "expert"), "tensor"),
        P(("dp", "expert"), "tensor"),
        P("expert", "dp", "tensor"),
    )
    return jax.shard_map(shards, mesh=mesh, in_specs=in_specs, out_specs=out_specs, check_vma=False)
```

time: 366 us -> 339 us (0.926)
  the two profiles are of different devices: /device:TPU:40 before, /device:TPU:1 now
where the time goes in v1:
time: 339 us; the launch traced here: 338 us
  blocking collectives  176 us (52%)
  waiting for transfers between devices  130 us (38%)
  between operations  13.8 us (4%)
  matrix products  12.2 us (4%)
  local copies, waits for them, and re-layouts  3.51 us (1%)
    all_to_all x1, blocking collectives, shards(): lax.all_to_all(send.reshape(experts, cap, -1), 'expert', split_axis=0, co...  92 us
    all_to_all x1, blocking collectives, shards(): lax.all_to_all(jnp.concatenate([out_rows, hidden_grad], axis=1).reshape(e...  83.8 us
    reduce_scatter x1, waiting for transfers between devices, shards(): lax.psum_scatter(partial_value, 'tensor', scatter_dimension=1, tiled=True)  69.2 us
    all_gather x1, waiting for transfers between devices, shards(): pieces = lax.all_gather(recv[:, cols:], 'tensor', axis=0, tiled=False)  61.2 us
  transfers between devices with their start and end apart: 3, of which 2 were waited for; matrix products, arithmetic and copies ran while one was open for 4% of the time, Pallas kernels for 0%

profile of v1, /device:TPU:1, one launch (start us, length us, event | category | flops | bytes accessed | tf_op | source)
XLA Modules:
  0.0 338.1 jit_solution(12277225397793052567)
XLA Ops:
  7.2 0.0 copy-start
  7.2 0.0 all-gather.3.cloned.1.call-start
  7.2 0.9 select_reduce_fusion.1
  8.1 0.1 fusion.19
  8.2 0.2 reduce_window_sum.11
  8.4 0.2 select_reduce_fusion
  8.6 0.0 copy-done
  8.6 1.2 fusion.7
  9.9 92.0 %all_to_all.10 = bf16[32,8,1152]{2,1,0:T(8,128)(2,1)S(1)} all-to-all(bf16[32,8,1152]{2,1,0:T(8,128)(2,1)S(1)} %fusion.7), channel_id=1, replica_groups=mesh['dp'=4,'expert'=32,'tensor'=8] {'expert'}, dimensions={0} | all-to-all | bytes 1179648 | tf_op jit(solution)/shard_map/all_to_all | solution.py:26
  101.8 0.7 slice.16
  102.5 0.0 all-gather.3.cloned.1.call-update
  102.5 0.0 reduce-scatter.3.cloned.1.call-start
  102.6 4.3 %fusion.4 = bf16[256,2048]{1,0:T(8,128)(2,1)} fusion(bf16[1,2048,896]{2,1,0:T(8,128)(2,1)} %param.7, bf16[256,1152]{1,0:T(8,128)(2,1)S(1)} %bitcast.28), kind=kOutput, calls=%fused_computation.5 | convolution fusion | flops 940048384 | bytes 5177344 | tf_op jit(solution)/shard_map/dot_general | solution.py:33
  106.9 0.0 reduce-scatter.3.cloned.1.call-update
  106.9 0.0 reduce-scatter.5.cloned.1.call-start
  107.0 61.2 %all-gather.3.cloned.1.call-done = bf16[2048,256]{1,0:T(8,128)(2,1)} async-done(((bf16[256,256]{1,0:T(8,128)(2,1)}), bf16[2048,256]{1,0:T(8,128)(2,1)}) %all-gather.3.cloned.1.call-update) | async-done | bytes 1048592 | tf_op jit(solution)/shard_map/all_gather | solution.py:30
  168.2 1.5 copy.8
  169.6 3.0 convolution_convert_fusion
  172.7 0.0 reduce-scatter.5.cloned.1.call-update
  172.7 3.3 fusion.8
  176.0 69.2 %reduce-scatter.3.cloned.1.call-done = bf16[256,256]{1,0:T(8,128)(2,1)} async-done(((bf16[256,2048]{1,0:T(8,128)(2,1)}), bf16[256,256]{1,0:T(8,128)(2,1)}) %reduce-scatter.3.cloned.1.call-update) | async-done | bytes 131088 | tf_op jit(solution)/shard_map/reduce_scatter | solution.py:36
  245.2 1.0 maximum_bitcast_fusion
  246.2 83.8 %all_to_all.11 = bf16[32,8,1152]{2,1,0:T(8,128)(2,1)S(1)} all-to-all(bf16[32,8,1152]{2,1,0:T(8,128)(2,1)S(1)} %maximum_bitcast_fusion), channel_id=1, replica_groups=mesh['dp'=4,'expert'=32,'tensor'=8] {'expert'}, dimensions={0} | all-to-all | bytes 1179648 | tf_op jit(solution)/shard_map/all_to_all | solution.py:38
  329.9 0.3 convolution_convert_fusion.2
  330.2 0.6 slice.19
  330.9 0.7 slice.18
  331.6 0.0 reduce-scatter.5.cloned.1.call-done
  (2 shorter events, 0.0 us)
Async XLA Ops:
  7.2 1.4 copy-start
  7.2 161.0 %all-gather.3.cloned.1.call-start = ((), (), s32[]{:S(2)}) async-start(), calls=%async_computation.6 | async-start | bytes 1179648 | tf_op jit(solution)/shard_map/all_gather | solution.py:30
  102.5 142.7 %reduce-scatter.3.cloned.1.call-start = ((), (), s32[]{:S(2)}) async-start(), calls=%async_computation.4 | async-start | bytes 1179648 | tf_op jit(solution)/shard_map/reduce_scatter | solution.py:36
  106.9 224.7 %reduce-scatter.5.cloned.1.call-start = ((), (), s32[]{:S(2)}) async-start(), calls=%async_computation.5 | async-start | bytes 4587520 | tf_op jit(solution)/shard_map/reduce_scatter | solution.py:48
Sparse Core Ops, SparseCore 0:
  102.6 65.4 all-gather.2
  171.6 73.6 reduce-scatter.2
  249.2 59.5 reduce-scatter.4

commit v2 on v1

v2 whole, which is shorter than its diff:
```python
import jax
import jax.numpy as jnp
from jax import lax
from jax.experimental import pallas as pl
from jax.experimental.pallas import tpu as pltpu
from jax.sharding import PartitionSpec as P

MESH = pl.DeviceIdType.MESH
F32 = jnp.float32
BF16 = jnp.bfloat16
NE = 32
CAP = 8
LINE = 8
UNITS = 24
SKEW = 3
SPLIT = 2
SKEW2 = 2


def exchange(
    send_h, send_g, w, out_recv, dh_recv, g_all, h_all,
    recv_h, recv_g, out_send, dh_send, partial, acc, plus_in, minus_in, plus_out, minus_out,
    g_ss, g_rs, o_ss, o_rs, d_ss, d_rs, h_ss, h_rs, x_ss, p_ss, p_rs, m_ss, m_rs,
    rp_ss, rp_rs, rm_ss, rm_rs, y_ss, y_rs, loc,
):
    e = lax.axis_index("expert")
    j = lax.axis_index("tensor")
    y = lax.axis_index("dp")
    width = send_h.shape[2]
    half = width // 2
    cols = send_g.shape[2]
    part = width // LINE
    quarter = width // 4
    x, h, c = e // 8, (e // 2) % 4, e % 2
    first, last = j == 0, j == LINE - 1

    def at(dx, dh, dc):
        return ((x + dx) % 4) * 8 + ((h + dh) % 4) * 2 + (c + dc) % 2

    def peer(k):
        q = k // 8
        dh = jnp.where(q == 0, 2, jnp.where(q == 1, 1, jnp.where(q == 2, 3, 0)))
        return at((k % 8) // 2, dh, k % 2)

    SELF = 24

    def others(fn):
        def step(k, carry):
            fn(k + (k >= SELF).astype(jnp.int32))
            return carry

        lax.fori_loop(0, NE - 1, step, 0)

    sign = jnp.where(last, 1, -1)
    far_end = jnp.where(last, 0, LINE - 1)
    at_end = jnp.logical_or(first, last)

    barrier = pltpu.get_barrier_semaphore()
    others(lambda k: pl.semaphore_signal(barrier, inc=1, device_id={"expert": peer(k)}, device_id_type=MESH))
    for d in (1, 2, 3):
        pl.semaphore_signal(barrier, inc=1, device_id={"dp": (y + d) % 4}, device_id_type=MESH)

    @pl.when(j > 0)
    def _():
        pl.semaphore_signal(barrier, inc=1, device_id={"tensor": j - 1}, device_id_type=MESH)

    @pl.when(j < LINE - 1)
    def _():
        pl.semaphore_signal(barrier, inc=1, device_id={"tensor": j + 1}, device_id_type=MESH)

    def partner(k):
        g = 1 + k // 8
        return ((k % 8) // 2) * 8 + ((h + sign * g + 8) % 4) * 2 + k % 2

    @pl.when(at_end)
    def _():
        def step(k, carry):
            pl.semaphore_signal(
                barrier, inc=1, device_id={"expert": partner(k), "tensor": far_end}, device_id_type=MESH
            )
            return carry

        lax.fori_loop(0, 16, step, 0)

    pl.semaphore_wait(barrier, 34 + (j > 0) + (j < LINE - 1) + jnp.where(at_end, 16, 0))

    def local(k, src, dst):
        return pltpu.make_async_copy(src, dst, loc.at[k])

    local(0, send_h.at[e], recv_h.at[e]).start()
    local(1, send_g.at[e], recv_g.at[e]).start()

    side = jnp.where(last, 0, 1)

    def export(k, recv):
        r, piece = k % 8, k // 8
        t = ((r // 2) * 8) + ((h + sign * jnp.where(piece == 0, 2, 1) + 8) % 4) * 2 + r % 2
        col = jnp.where(piece == 0, side, piece - 1)
        mine = x * 2 + c
        unit = jnp.where(piece == 0, 16 + mine, mine * 2 + piece - 1)
        span = pl.ds(pl.multiple_of(col * half, half), half)
        return pltpu.make_async_remote_copy(
            src_ref=send_h.at[t, :, span],
            dst_ref=recv_h.at[e, :, span],
            send_sem=x_ss.at[k],
            recv_sem=recv.at[unit],
            device_id={"expert": t, "tensor": far_end},
            device_id_type=MESH,
        )

    def run(count, fn):
        def step(k, carry):
            fn(k)
            return carry

        lax.fori_loop(0, count, step, 0)

    @pl.when(last)
    def _():
        run(UNITS, lambda k: export(k, p_rs).start())

    @pl.when(first)
    def _():
        run(UNITS, lambda k: export(k, m_rs).start())

    def near(k):
        t = at(k // 2, 0, k % 2)
        return pltpu.make_async_remote_copy(
            src_ref=send_h.at[t],
            dst_ref=recv_h.at[e],
            send_sem=h_ss.at[k],
            recv_sem=h_rs.at[x * 2 + c],
            device_id={"expert": t},
            device_id_type=MESH,
        )

    run(7, lambda k: near(k + 1).start())

    def spread(src, dst, ss, rs):
        def copy(k):
            t = peer(k)
            return pltpu.make_async_remote_copy(
                src_ref=src.at[t],
                dst_ref=dst.at[e],
                send_sem=ss.at[k],
                recv_sem=rs.at[e],
                device_id={"expert": t},
                device_id_type=MESH,
            )

        return copy

    def arrivals(dst, rs):
        def copy(k):
            t = peer(k)
            pltpu.make_async_copy(dst.at[t], dst.at[t], rs.at[t]).wait()

        return copy

    grads = spread(send_g, recv_g, g_ss, g_rs)
    others(lambda k: grads(k).start())

    def relay(u, up):
        ss, rs = (p_ss, p_rs) if up else (m_ss, m_rs)
        wide = u < 16
        idx = jnp.where(wide, u // 2, u - 16)
        col = jnp.where(wide, u % 2, 0 if up else 1)
        hop = jnp.where(wide, 1, 2)
        g = (h - hop + 4) % 4 if up else (h + hop) % 4
        s = (idx // 2) * 8 + g * 2 + idx % 2
        ref = recv_h.at[s, :, pl.ds(pl.multiple_of(col * half, half), half)]
        return pltpu.make_async_remote_copy(
            src_ref=ref,
            dst_ref=ref,
            send_sem=ss.at[u],
            recv_sem=rs.at[u],
            device_id={"tensor": (j + 1) % LINE if up else (j + LINE - 1) % LINE},
            device_id_type=MESH,
        )

    def relay_step(tau):
        for up in (True, False):
            u = tau - SKEW * (j if up else LINE - 1 - j)

            @pl.when(jnp.logical_and(u >= 0, u < UNITS))
            def _(u=u, up=up):
                copy = relay(u, up)
                copy.wait_recv()

                @pl.when(j < LINE - 1 if up else j > 0)
                def _():
                    copy.start()

    run(UNITS + SKEW * (LINE - 1), relay_step)

    local(0, send_h.at[e], recv_h.at[e]).wait()

    def near_in(k):
        t = at((k + 1) // 2, 0, (k + 1) % 2)
        ref = recv_h.at[t]
        pltpu.make_async_copy(ref, ref, h_rs.at[(t // 8) * 2 + t % 2]).wait()

    run(7, near_in)

    def hid_y(d):
        t = (y + d) % 4
        return pltpu.make_async_remote_copy(
            src_ref=recv_h.at[:, :, pl.ds(pl.multiple_of(t * quarter, quarter), quarter)],
            dst_ref=h_all.at[y],
            send_sem=y_ss.at[d],
            recv_sem=y_rs.at[y],
            device_id={"dp": t},
            device_id_type=MESH,
        )

    def grad_y(d):
        return pltpu.make_async_remote_copy(
            src_ref=recv_g,
            dst_ref=g_all.at[y],
            send_sem=y_ss.at[4 + d],
            recv_sem=y_rs.at[4 + y],
            device_id={"dp": (y + d) % 4},
            device_id_type=MESH,
        )

    own_h = recv_h.at[:, :, pl.ds(pl.multiple_of(y * quarter, quarter), quarter)]
    for d in (2, 1, 3):
        hid_y(d).start()
    local(2, own_h, h_all.at[y]).start()

    rows = NE * CAP

    def project(start, size):
        span = pl.ds(start, size)
        value = jnp.dot(recv_h[...].reshape(rows, width), w[:, span], preferred_element_type=F32)
        out_send[:, :, span] = value.astype(BF16).reshape(NE, CAP, size)

    run(cols // 256, lambda k: project(pl.multiple_of(k * 256, 256), 256))
    if cols % 256:
        project(cols - cols % 256, cols % 256)
    outs = spread(out_send, out_recv, o_ss, o_rs)
    others(lambda k: outs(k).start())
    local(3, out_send.at[e], out_recv.at[e]).start()

    local(1, send_g.at[e], recv_g.at[e]).wait()
    others(arrivals(recv_g, g_rs))
    for d in (2, 1, 3):
        grad_y(d).start()
    local(4, recv_g, g_all.at[y]).start()

    def chunk(d):
        value = lax.dot_general(
            recv_g[...].reshape(rows, cols),
            w[pl.ds(pl.multiple_of(d * part, part), part), :],
            (((1,), (1,)), ((), ())),
            preferred_element_type=F32,
        )
        partial[d] = value

    run(LINE, chunk)
    acc[...] = partial[j]
    piece = rows // SPLIT

    def passing(m, up):
        inn, out, ss, rs = (plus_in, plus_out, rp_ss, rp_rs) if up else (minus_in, minus_out, rm_ss, rm_rs)
        return pltpu.make_async_remote_copy(
            src_ref=out.at[m],
            dst_ref=inn.at[m],
            send_sem=ss.at[m],
            recv_sem=rs.at[m],
            device_id={"tensor": (j + 1) % LINE if up else (j + LINE - 1) % LINE},
            device_id_type=MESH,
        )

    def reduce_step(tau):
        for up in (True, False):
            lag = j if up else LINE - 1 - j
            inn, out = (plus_in, plus_out) if up else (minus_in, minus_out)
            m = tau - SKEW2 * lag
            count = SPLIT * (LINE - lag)

            @pl.when(jnp.logical_and(m >= 0, m < count))
            def _(m=m, up=up, lag=lag, inn=inn, out=out, count=count):
                copy = passing(m, up)
                d = LINE - 1 - m // SPLIT if up else m // SPLIT
                span = pl.ds(pl.multiple_of((m % SPLIT) * piece, piece), piece)
                final = m >= count - SPLIT

                @pl.when(lag > 0)
                def _():
                    copy.wait_recv()

                    @pl.when(final)
                    def _():
                        acc[span, :] += inn[m].astype(F32)

                    @pl.when(jnp.logical_not(final))
                    def _():
                        out[m] = (partial[d, span, :] + inn[m].astype(F32)).astype(BF16)

                @pl.when(lag == 0)
                def _():
                    out[m] = partial[d, span, :].astype(BF16)

                @pl.when(jnp.logical_not(final))
                def _():
                    copy.start()

    run(max(SPLIT * (LINE - k) + SKEW2 * k for k in range(LINE)), reduce_step)
    dh_send[...] = acc[...].astype(BF16).reshape(NE, CAP, part)
    backs = spread(dh_send, dh_recv, d_ss, d_rs)
    others(lambda k: backs(k).start())
    local(5, dh_send.at[e], dh_recv.at[e]).start()

    local(2, own_h, h_all.at[y]).wait()
    local(3, out_send.at[e], out_recv.at[e]).wait()
    local(4, recv_g, g_all.at[y]).wait()
    local(5, dh_send.at[e], dh_recv.at[e]).wait()
    others(lambda k: grads(k).wait_send())
    others(lambda k: outs(k).wait_send())
    run(7, lambda k: near(k + 1).wait_send())

    @pl.when(last)
    def _():
        run(UNITS, lambda k: export(k, p_rs).wait_send())

    @pl.when(first)
    def _():
        run(UNITS, lambda k: export(k, m_rs).wait_send())

    @pl.when(j < LINE - 1)
    def _():
        run(UNITS, lambda u: relay(u, True).wait_send())
        run(SPLIT * (LINE - 1 - j), lambda m: passing(m, True).wait_send())

    @pl.when(j > 0)
    def _():
        run(UNITS, lambda u: relay(u, False).wait_send())
        run(SPLIT * j, lambda m: passing(m, False).wait_send())

    for d in (1, 2, 3):
        hid_y(d).wait_send()
        grad_y(d).wait_send()
        t = (y + d) % 4
        pltpu.make_async_copy(h_all.at[t], h_all.at[t], y_rs.at[t]).wait()
        pltpu.make_async_copy(g_all.at[t], g_all.at[t], y_rs.at[4 + t]).wait()
    others(arrivals(out_recv, o_rs))
    others(lambda k: backs(k).wait_send())
    others(arrivals(dh_recv, d_rs))


def shards(hidden, out_grad, w_down, routes, placement):
    experts = lax.axis_size("expert")
    replicas = lax.axis_size("dp")
    tok, width = hidden.shape
    cols = out_grad.shape[1]
    slots = experts * CAP
    part = width // LINE
    chosen = routes == jnp.arange(placement.shape[0], dtype=jnp.int32)[None, :]
    target = jnp.sum(jnp.where(chosen, placement[None, :], 0), axis=1)
    landing = target[:, None] == jnp.arange(experts, dtype=jnp.int32)[None, :]
    counted = jnp.cumsum(landing.astype(jnp.int32), axis=0) - 1
    within = jnp.sum(jnp.where(landing, counted, 0), axis=1)
    position = target * CAP + within
    picker = (jnp.arange(slots, dtype=jnp.int32)[:, None] == position[None, :]).astype(BF16)
    send_hidden = jnp.dot(picker, hidden, preferred_element_type=F32).astype(BF16)
    send_grad = jnp.dot(picker, out_grad, preferred_element_type=F32).astype(BF16)
    vmem = pl.BlockSpec(memory_space=pltpu.VMEM)
    dma = pltpu.SemaphoreType.DMA
    piece = (SPLIT * LINE, slots // SPLIT, part)
    back_out, back_grad, g_all, h_all = pl.pallas_call(
        exchange,
        out_shape=(
            jax.ShapeDtypeStruct((experts, CAP, cols), BF16),
            jax.ShapeDtypeStruct((experts, CAP, part), BF16),
            jax.ShapeDtypeStruct((replicas, experts, CAP, cols), BF16),
            jax.ShapeDtypeStruct((replicas, experts, CAP, width // replicas), BF16),
        ),
        in_specs=[vmem] * 3,
        out_specs=(vmem,) * 4,
        scratch_shapes=[
            pltpu.VMEM((experts, CAP, width), BF16),
            pltpu.VMEM((experts, CAP, cols), BF16),
            pltpu.VMEM((experts, CAP, cols), BF16),
            pltpu.VMEM((experts, CAP, part), BF16),
            pltpu.VMEM((LINE, slots, part), F32),
            pltpu.VMEM((slots, part), F32),
            pltpu.VMEM(piece, BF16),
            pltpu.VMEM(piece, BF16),
            pltpu.VMEM(piece, BF16),
            pltpu.VMEM(piece, BF16),
            *[dma((NE,))] * 6,
            *[dma((8,))] * 2,
            *[dma((UNITS,))] * 5,
            *[dma((SPLIT * LINE,))] * 4,
            *[dma((8,))] * 2,
            dma((6,)),
        ],
        compiler_params=pltpu.CompilerParams(collective_id=0, has_side_effects=True, vmem_limit_bytes=40 * 2**20),
        name="exchange",
    )(send_hidden.reshape(experts, CAP, width), send_grad.reshape(experts, CAP, cols), w_down[0])
    output = jnp.einsum("rt,rd->td", picker, back_out.reshape(slots, cols), preferred_element_type=F32).astype(BF16)
    d_hidden = jnp.einsum("rt,rd->td", picker, back_grad.reshape(slots, part), preferred_element_type=F32).astype(BF16)
    d_weight = lax.dot_general(
        h_all.reshape(replicas * slots, -1),
        g_all.reshape(replicas * slots, cols),
        (((0,), (0,)), ((), ())),
        preferred_element_type=F32,
    ).astype(BF16)
    return (output, d_hidden, d_weight[None])


def solution(mesh):
    in_specs = (
        P(("dp", "expert"), None),
        P(("dp", "expert"), "tensor"),
        P("expert", None, "tensor"),
        P(("dp", "expert"), None),
        P(),
    )
    out_specs = (
        P(("dp", "expert"), "tensor"),
        P(("dp", "expert"), "tensor"),
        P("expert", "dp", "tensor"),
    )
    return jax.shard_map(shards, mesh=mesh, in_specs=in_specs, out_specs=out_specs, check_vma=False)
```

time: 339 us -> 215 us (0.63)
  Pallas kernels: 0 us -> 205 us
  blocking collectives: 176 us -> 0 us
  waiting for transfers between devices: 130 us -> 0 us
  between operations: 13.8 us -> 0.71 us
  matrix products: 12.2 us -> 5.65 us
    pallas_call x0 -> x1, Pallas kernels: none -> 205 us  [shards(): pl.pallas_call(exchange, out_shape=(jax.ShapeDtypeStruct((experts, CAP, c...]
    all_to_all x2 -> x0, blocking collectives: 176 us -> none  [the longest x1 92 us: shards(): lax.all_to_all(send.reshape(experts, cap, -1), 'expert', split_axis=0, co...]
    reduce_scatter x2 -> x0, waiting for transfers between devices: 69.2 us -> none  [the longest x1 69.2 us: shards(): lax.psum_scatter(partial_value, 'tensor', scatter_dimension=1, tiled=True)]
    all_gather x1 -> x0, waiting for transfers between devices: 61.2 us -> none  [shards(): pieces = lax.all_gather(recv[:, cols:], 'tensor', axis=0, tiled=False)]
    dot_general x5, matrix products: 12.2 us -> 5.65 us  [the longest x1 2.21 us: shards(): lax.dot_general(h_all.reshape(replicas * slots, -1), g_all.reshape(replic...]
  transfers between devices with their start and end apart: 3 -> 0, of which waited for: 2 -> 0; matrix products, arithmetic and copies ran while one was open for 4% -> 0% of each run, Pallas kernels for 0% -> 0%
where the time goes in v2:
time: 215 us; the launch traced here: 214 us
  Pallas kernels  205 us (95%)
  matrix products  5.65 us (3%)
    pallas_call x1, Pallas kernels, shards(): pl.pallas_call(exchange, out_shape=(jax.ShapeDtypeStruct((experts, CAP, c...  205 us

profile of v2, /device:TPU:1, one launch (start us, length us, event | category | flops | bytes accessed | tf_op | source)
XLA Modules:
  0.0 214.4 jit_solution(4443659685686410600)
XLA Ops:
  0.6 0.0 copy-start
  0.6 0.9 select_reduce_fusion.1
  1.6 0.1 fusion.9
  1.6 0.2 reduce_window_sum.11
  1.8 0.2 select_reduce_fusion
  2.0 1.2 fusion.2.send_g
  3.2 0.0 copy-done
  3.2 0.4 fusion.send_h
  3.7 0.0 copy-start.1
  3.7 2.0 copy-done.1
  5.7 204.6 %exchange.1 = (bf16[32,8,896]{2,1,0:T(8,128)(2,1)S(1)}, bf16[32,8,256]{2,1,0:T(8,128)(2,1)S(1)}, bf16[4,32,8,896]{3,2,1,0:T(8,128)(2,1)S(1)}, bf16[4,32,8,512]{3,2,1,0:T(8,128)(2,1)S(1)}) custom-call(bf16[32,8,2048]{2,1,0:T(8,128)(2,1)S(1)} %fusion.send_h, bf16[32,8,896]{2,1,0:T(8,128)(2,1)S(1)} %fusion.2.send_g, bf16[2048,896]{1,0:T(8,128)(2,1)S(1)} %bitcast.24), custom_call_target="tpu_custom_call" | custom-call | tf_op jit(solution)/shard_map/exchange/pallas_call | solution.py:371
  210.4 1.0 convolution_convert_fusion.2
  211.3 0.9 convolution_convert_fusion.3
  212.2 2.2 %fusion.1 = bf16[1,512,896]{2,1,0:T(8,128)(2,1)} fusion(bf16[4,32,8,512]{3,2,1,0:T(8,128)(2,1)S(1)} %get-tuple-element.9, bf16[4,32,8,896]{3,2,1,0:T(8,128)(2,1)S(1)} %get-tuple-element.10), kind=kOutput, calls=%fused_computation.3 | convolution fusion | flops 939982848 | bytes 3801088 | tf_op jit(solution)/shard_map/dot_general | solution.py:404
  (1 shorter events, 0.0 us)
Async XLA Ops:
  0.6 2.6 %copy-start = (bf16[128,2048]{1,0:T(8,128)(2,1)S(1)}, bf16[128,2048]{1,0:T(8,128)(2,1)}, u32[]{:S(2)}) copy-start(bf16[128,2048]{1,0:T(8,128)(2,1)} %param.5) | copy-start | bytes 1572868
  3.7 2.0 copy-start.1

commit v3 on v2

--- a/solution.py
+++ b/solution.py
@@ -12,20 +12,24 @@
 CAP = 8
 LINE = 8
 UNITS = 24
-SKEW = 3
+SKEW = 5
 SPLIT = 2
 SKEW2 = 2
+START = 30
+EXPORT_FIRST = True
 
 
 def exchange(
-    send_h, send_g, w, out_recv, dh_recv, g_all, h_all,
-    recv_h, recv_g, out_send, dh_send, partial, acc, plus_in, minus_in, plus_out, minus_out,
+    hidden, out_grad, picker, w_any, out_recv, dh_recv, g_all, h_all,
+    send_h, send_g, w, recv_h, recv_g, out_send, dh_send, partial, acc, plus_in, minus_in, plus_out, minus_out,
     g_ss, g_rs, o_ss, o_rs, d_ss, d_rs, h_ss, h_rs, x_ss, p_ss, p_rs, m_ss, m_rs,
     rp_ss, rp_rs, rm_ss, rm_rs, y_ss, y_rs, loc,
 ):
     e = lax.axis_index("expert")
     j = lax.axis_index("tensor")
     y = lax.axis_index("dp")
+    local_w = pltpu.make_async_copy(w_any, w, loc.at[6])
+    local_w.start()
     width = send_h.shape[2]
     half = width // 2
     cols = send_g.shape[2]
@@ -82,6 +86,23 @@
 
         lax.fori_loop(0, 16, step, 0)
 
+    def pick(src, dst, start, size):
+        span = pl.ds(start, size)
+        value = jnp.dot(picker[...], src[:, span], preferred_element_type=F32)
+        dst[:, :, span] = value.astype(BF16).reshape(NE, CAP, size)
+
+    def pick_all(src, dst, total):
+        def step(k, carry):
+            pick(src, dst, pl.multiple_of(k * 256, 256), 256)
+            return carry
+
+        lax.fori_loop(0, total // 256, step, 0)
+        if total % 256:
+            pick(src, dst, total - total % 256, total % 256)
+
+    pick_all(hidden, send_h, width)
+    pick_all(out_grad, send_g, cols)
+
     pl.semaphore_wait(barrier, 34 + (j > 0) + (j < LINE - 1) + jnp.where(at_end, 16, 0))
 
     def local(k, src, dst):
@@ -115,14 +136,6 @@
 
         lax.fori_loop(0, count, step, 0)
 
-    @pl.when(last)
-    def _():
-        run(UNITS, lambda k: export(k, p_rs).start())
-
-    @pl.when(first)
-    def _():
-        run(UNITS, lambda k: export(k, m_rs).start())
-
     def near(k):
         t = at(k // 2, 0, k % 2)
         return pltpu.make_async_remote_copy(
@@ -134,7 +147,14 @@
             device_id_type=MESH,
         )
 
-    run(7, lambda k: near(k + 1).start())
+    def exports():
+        @pl.when(last)
+        def _():
+            run(UNITS, lambda k: export(k, p_rs).start())
+
+        @pl.when(first)
+        def _():
+            run(UNITS, lambda k: export(k, m_rs).start())
 
     def spread(src, dst, ss, rs):
         def copy(k):
@@ -158,7 +178,12 @@
         return copy
 
     grads = spread(send_g, recv_g, g_ss, g_rs)
+    if EXPORT_FIRST:
+        exports()
     others(lambda k: grads(k).start())
+    if not EXPORT_FIRST:
+        exports()
+    run(7, lambda k: near(k + 1).start())
 
     def relay(u, up):
         ss, rs = (p_ss, p_rs) if up else (m_ss, m_rs)
@@ -191,16 +216,10 @@
                 def _():
                     copy.start()
 
-    run(UNITS + SKEW * (LINE - 1), relay_step)
-
-    local(0, send_h.at[e], recv_h.at[e]).wait()
-
     def near_in(k):
         t = at((k + 1) // 2, 0, (k + 1) % 2)
         ref = recv_h.at[t]
         pltpu.make_async_copy(ref, ref, h_rs.at[(t // 8) * 2 + t % 2]).wait()
-
-    run(7, near_in)
 
     def hid_y(d):
         t = (y + d) % 4
@@ -224,10 +243,6 @@
         )
 
     own_h = recv_h.at[:, :, pl.ds(pl.multiple_of(y * quarter, quarter), quarter)]
-    for d in (2, 1, 3):
-        hid_y(d).start()
-    local(2, own_h, h_all.at[y]).start()
-
     rows = NE * CAP
 
     def project(start, size):
@@ -235,18 +250,19 @@
         value = jnp.dot(recv_h[...].reshape(rows, width), w[:, span], preferred_element_type=F32)
         out_send[:, :, span] = value.astype(BF16).reshape(NE, CAP, size)
 
-    run(cols // 256, lambda k: project(pl.multiple_of(k * 256, 256), 256))
-    if cols % 256:
-        project(cols - cols % 256, cols % 256)
     outs = spread(out_send, out_recv, o_ss, o_rs)
-    others(lambda k: outs(k).start())
-    local(3, out_send.at[e], out_recv.at[e]).start()
-
-    local(1, send_g.at[e], recv_g.at[e]).wait()
-    others(arrivals(recv_g, g_rs))
-    for d in (2, 1, 3):
-        grad_y(d).start()
-    local(4, recv_g, g_all.at[y]).start()
+
+    def forward():
+        local(0, send_h.at[e], recv_h.at[e]).wait()
+        run(7, near_in)
+        run(cols // 256, lambda k: project(pl.multiple_of(k * 256, 256), 256))
+        if cols % 256:
+            project(cols - cols % 256, cols % 256)
+        others(lambda k: outs(k).start())
+        local(3, out_send.at[e], out_recv.at[e]).start()
+        for d in (2, 1, 3):
+            hid_y(d).start()
+        local(2, own_h, h_all.at[y]).start()
 
     def chunk(d):
         value = lax.dot_general(
@@ -257,8 +273,15 @@
         )
         partial[d] = value
 
-    run(LINE, chunk)
-    acc[...] = partial[j]
+    def backward():
+        local(1, send_g.at[e], recv_g.at[e]).wait()
+        others(arrivals(recv_g, g_rs))
+        run(LINE, chunk)
+        acc[...] = partial[j]
+        for d in (2, 1, 3):
+            grad_y(d).start()
+        local(4, recv_g, g_all.at[y]).start()
+
     piece = rows // SPLIT
 
     def passing(m, up):
@@ -306,7 +329,24 @@
                 def _():
                     copy.start()
 
-    run(max(SPLIT * (LINE - k) + SKEW2 * k for k in range(LINE)), reduce_step)
+    relay_end = UNITS + SKEW * (LINE - 1)
+    own_end = UNITS + SKEW * jnp.maximum(j, LINE - 1 - j)
+    reduce_end = START + max(SPLIT * (LINE - k) + SKEW2 * k for k in range(LINE))
+
+    def both(tau):
+        @pl.when(tau == START)
+        def _():
+            backward()
+
+        @pl.when(tau == own_end)
+        def _():
+            forward()
+
+        relay_step(tau)
+        reduce_step(tau - START)
+
+    local_w.wait()
+    run(max(relay_end + 1, reduce_end), both)
     dh_send[...] = acc[...].astype(BF16).reshape(NE, CAP, part)
     backs = spread(dh_send, dh_recv, d_ss, d_rs)
     others(lambda k: backs(k).start())
@@ -363,8 +403,6 @@
     within = jnp.sum(jnp.where(landing, counted, 0), axis=1)
     position = target * CAP + within
     picker = (jnp.arange(slots, dtype=jnp.int32)[:, None] == position[None, :]).astype(BF16)
-    send_hidden = jnp.dot(picker, hidden, preferred_element_type=F32).astype(BF16)
-    send_grad = jnp.dot(picker, out_grad, preferred_element_type=F32).astype(BF16)
     vmem = pl.BlockSpec(memory_space=pltpu.VMEM)
     dma = pltpu.SemaphoreType.DMA
     piece = (SPLIT * LINE, slots // SPLIT, part)
@@ -376,9 +414,12 @@
             jax.ShapeDtypeStruct((replicas, experts, CAP, cols), BF16),
             jax.ShapeDtypeStruct((replicas, experts, CAP, width // replicas), BF16),
         ),
-        in_specs=[vmem] * 3,
+        in_specs=[vmem] * 3 + [pl.BlockSpec(memory_space=pl.ANY)],
         out_specs=(vmem,) * 4,
         scratch_shapes=[
+            pltpu.VMEM((experts, CAP, width), BF16),
+            pltpu.VMEM((experts, CAP, cols), BF16),
+            pltpu.VMEM((width, cols), BF16),
             pltpu.VMEM((experts, CAP, width), BF16),
             pltpu.VMEM((experts, CAP, cols), BF16),
             pltpu.VMEM((experts, CAP, cols), BF16),
@@ -394,11 +435,11 @@
             *[dma((UNITS,))] * 5,
             *[dma((SPLIT * LINE,))] * 4,
             *[dma((8,))] * 2,
-            dma((6,)),
+            dma((7,)),
         ],
-        compiler_params=pltpu.CompilerParams(collective_id=0, has_side_effects=True, vmem_limit_bytes=40 * 2**20),
+        compiler_params=pltpu.CompilerParams(collective_id=0, has_side_effects=True, vmem_limit_bytes=60 * 2**20),
         name="exchange",
-    )(send_hidden.reshape(experts, CAP, width), send_grad.reshape(experts, CAP, cols), w_down[0])
+    )(hidden, out_grad, picker, w_down[0])
     output = jnp.einsum("rt,rd->td", picker, back_out.reshape(slots, cols), preferred_element_type=F32).astype(BF16)
     d_hidden = jnp.einsum("rt,rd->td", picker, back_grad.reshape(slots, part), preferred_element_type=F32).astype(BF16)
     d_weight = lax.dot_general(

time: 215 us -> 204 us (0.949)
  Pallas kernels: 205 us -> 194 us
    pallas_call x1, Pallas kernels: 205 us -> 194 us  [shards(): pl.pallas_call(exchange, out_shape=(jax.ShapeDtypeStruct((experts, CAP, c...]
where the time goes in v3:
time: 204 us
  Pallas kernels  194 us (95%)
  matrix products  7.77 us (4%)
    pallas_call x1, Pallas kernels, shards(): pl.pallas_call(exchange, out_shape=(jax.ShapeDtypeStruct((experts, CAP, c...  194 us

profile of v3, /device:TPU:1, one launch (start us, length us, event | category | flops | bytes accessed | tf_op | source)
XLA Modules:
  0.0 204.0 jit_solution(16958819798156071247)
XLA Ops:
  0.6 0.8 select_reduce_fusion.1
  1.5 0.1 fusion.6
  1.6 0.2 reduce_window_sum.11
  1.8 0.2 select_reduce_fusion
  1.9 0.7 fusion.3.picker
  2.6 193.6 %exchange.1 = (bf16[32,8,896]{2,1,0:T(8,128)(2,1)}, bf16[32,8,256]{2,1,0:T(8,128)(2,1)}, bf16[4,32,8,896]{3,2,1,0:T(8,128)(2,1)}, bf16[4,32,8,512]{3,2,1,0:T(8,128)(2,1)}) custom-call(bf16[128,2048]{1,0:T(8,128)(2,1)} %hidden.1, bf16[128,896]{1,0:T(8,128)(2,1)} %out_grad.1, bf16[256,128]{1,0:T(8,128)(2,1)} %fusion.3.picker, bf16[2048,896]{1,0:T(8,128)(2,1)} %bitcast.18), custom_call_target="tpu_custom_call" | custom-call | tf_op jit(solution)/shard_map/exchange/pallas_call | solution.py:409
  196.2 2.0 convolution_convert_fusion
  198.2 1.8 convolution_convert_fusion.1
  199.9 4.0 %fusion = bf16[1,512,896]{2,1,0:T(8,128)(2,1)} fusion(bf16[4,32,8,512]{3,2,1,0:T(8,128)(2,1)} %get-tuple-element.9, bf16[4,32,8,896]{3,2,1,0:T(8,128)(2,1)} %get-tuple-element.10), kind=kOutput, calls=%fused_computation.1 | convolution fusion | flops 939982848 | bytes 3801088 | tf_op jit(solution)/shard_map/dot_general | solution.py:445
  (1 shorter events, 0.0 us)
